TPU v7x, 32 devices: a whole 2x2x4 slice. The times are simulated.
32 devices in a mesh: chan: 8 (over z, y), grp: 4 (over x, core).
Axes of the slice: x: 2, y: 2, z: 4, core: 2. Of those that a mesh axis runs over, the one named last changes fastest.
Arguments:
- eta_pp: bfloat16 [32, 640, 640], P(('chan', 'grp'))
- ham_pp: bfloat16 [32, 640, 640], P(('chan', 'grp'))
- pp_factor: float32 [32, 640], P(('chan', 'grp')), may hold values from -1 to 1
- ph_factor: float32 [32, 640], P(('chan', 'grp')), may hold values from -1 to 1
- channel_size: int32 [32], P(('chan', 'grp')), may hold values from 320 to 640, as said below
- dest_dev: int32 [32, 160], P(('chan', 'grp')), may hold values from 0 to 7, as said below
- dest_sub: int32 [32, 160], P(('chan', 'grp')), may hold values from 0 to 159, as said below
- col_map: int32 [32, 640], P(('chan', 'grp')), may hold values from 0 to 639, each once within a row
- pair_swap: int32 [32, 640], P(('chan', 'grp')), may hold values from 0 to 639, as said below
Outputs:
- pp_flow: float32 [32, 640, 640], P(('chan', 'grp'))
- energy_flow: float32 [], replicated
Inputs may be any that keep to these rules, and one draw needn't show every extreme that they name: `channel_size`: a multiple of 4. `dest_dev`: every ph channel receives each of its 160 positions from exactly one pp subblock of its own group; from one pp channel at most 20 subblocks go to one ph channel, and exactly 20 for some. `dest_sub`: for each ph channel the positions it receives are all different. `pair_swap`: an involution of each channel's pairs without fixed points.
All inputs are finite; a program needn't handle non-finite values.
Results may differ from a plain program's by a relative error of at most 0.0036.
Values may be sent and summed in bfloat16 or wider, within the bound.
No kernel may reach another device: no remote copies, remote signals or barrier semaphores. Data moves between devices by JAX's collectives and lax.ppermute only.
A program may use at most 64 MiB of HBM per device.

v0:
```python
import jax
import jax.numpy as jnp
from jax import lax
from jax.sharding import PartitionSpec as P


def scaled_rows(scale, matrix):
    return (scale[:, None] * matrix.astype(jnp.float32)).astype(jnp.bfloat16)


def commutator(left, right, scale):
    return jnp.dot(left, scaled_rows(scale, right), preferred_element_type=jnp.float32) - jnp.dot(
        right, scaled_rows(scale, left), preferred_element_type=jnp.float32
    )


def on_device(
    eta_pp, ham_pp, pp_factor, ph_factor, channel_size, dest_dev, dest_sub, col_map, pair_swap
):
    width_cap = eta_pp.shape[1]
    peer_count = lax.axis_size("chan")
    sub_count = dest_dev.shape[1]
    strip_rows = width_cap // sub_count
    slot_count = (sub_count + peer_count - 1) // peer_count
    slot_total = peer_count * slot_count
    row_len = strip_rows * width_cap
    pair_index = jnp.arange(width_cap, dtype=jnp.int32)
    living = pair_index < channel_size[0]
    inside = living[:, None] & living[None, :]
    zero_half = jnp.zeros((), jnp.bfloat16)
    gen_masked = jnp.where(inside, eta_pp[0], zero_half)
    ham_masked = jnp.where(inside, ham_pp[0], zero_half)
    pp_scale = pp_factor[0]
    targets = dest_dev[0]
    blocks = jnp.arange(sub_count, dtype=jnp.int32)
    earlier = (targets[:, None] == targets[None, :]) & (blocks[None, :] < blocks[:, None])
    ranking = jnp.sum(earlier.astype(jnp.int32), axis=1)
    placing = targets * slot_count + ranking
    slot_source = jnp.full((slot_total,), sub_count, jnp.int32).at[placing].set(blocks)
    slot_valid = (slot_source < sub_count)[:, None]
    slot_index = jnp.minimum(slot_source, sub_count - 1)

    def pack_rows(matrix):
        strips = matrix.reshape(sub_count, row_len)
        buffer = jnp.where(slot_valid, jnp.take(strips, slot_index, axis=0), zero_half)
        return buffer.reshape(peer_count, slot_count, row_len)

    positions = jnp.where(slot_source < sub_count, jnp.take(dest_sub[0], slot_index), sub_count)
    positions = positions.reshape(peer_count, slot_count)
    columns = col_map[0]
    gen_recv, got_pos = (
        lax.all_to_all(pack_rows(gen_masked), "chan", split_axis=0, concat_axis=0, tiled=True),
        lax.all_to_all(positions, "chan", split_axis=0, concat_axis=0, tiled=True),
    )
    ham_recv = lax.all_to_all(
        pack_rows(ham_masked), "chan", split_axis=0, concat_axis=0, tiled=True
    )
    flat_pos = got_pos.reshape(-1)
    arrival = (
        jnp.zeros((sub_count,), jnp.int32)
        .at[flat_pos]
        .set(jnp.arange(slot_total, dtype=jnp.int32), mode="drop")
    )

    def place_rows(received):
        rows = received.reshape(slot_total, row_len)
        whole = jnp.take(rows, arrival, axis=0)
        return jnp.take(whole.reshape(width_cap, width_cap), columns, axis=1)

    gen_ph = place_rows(gen_recv)
    ham_ph = place_rows(ham_recv)
    ph_comm = commutator(gen_ph, ham_ph, ph_factor[0]).astype(jnp.bfloat16)
    inverse_cols = jnp.zeros((width_cap,), jnp.int32).at[columns].set(pair_index)
    unperm = jnp.take(ph_comm, inverse_cols, axis=1)
    strips = unperm.reshape(sub_count, row_len)
    picked = jnp.take(strips, jnp.minimum(flat_pos, sub_count - 1), axis=0)
    picked = jnp.where((flat_pos < sub_count)[:, None], picked, zero_half)
    returned = lax.all_to_all(
        picked.reshape(peer_count, slot_count, row_len),
        "chan",
        split_axis=0,
        concat_axis=0,
        tiled=True,
    )
    back_half = jnp.take(returned.reshape(slot_total, row_len), placing, axis=0).reshape(
        width_cap, width_cap
    )
    ladder = commutator(gen_masked, ham_masked, pp_scale)
    partner = pair_swap[0]
    row_swapped = jnp.take(back_half, partner, axis=0)
    col_swapped = jnp.take(back_half, partner, axis=1)
    both_swapped = jnp.take(row_swapped, partner, axis=1)
    anti = (
        back_half.astype(jnp.float32)
        - row_swapped.astype(jnp.float32)
        - col_swapped.astype(jnp.float32)
        + both_swapped.astype(jnp.float32)
    )
    flow = jnp.where(inside, 0.5 * ladder + anti, jnp.zeros((), jnp.float32))
    energy_flow = 0.25 * lax.psum(jnp.trace(ladder), ("chan", "grp"))
    return (flow[None], energy_flow)


def solution(mesh):
    in_specs = (
        P(("chan", "grp"), None, None),
        P(("chan", "grp"), None, None),
        P(("chan", "grp"), None),
        P(("chan", "grp"), None),
        P(("chan", "grp")),
        P(("chan", "grp"), None),
        P(("chan", "grp"), None),
        P(("chan", "grp"), None),
        P(("chan", "grp"), None),
    )
    out_specs = (P(("chan", "grp"), None, None), P())
    return jax.shard_map(
        on_device, mesh=mesh, in_specs=in_specs, out_specs=out_specs, check_vma=False
    )
```

profile of v0, /device:TPU:12, one launch (start us, length us, event | category | flops | bytes accessed | tf_op | source)
XLA Modules:
  0.0 191.2 jit_solution(12295517832593732478)
XLA Ops:
  3.4 1.6 gather_fusion
  5.8 6.2 %all-to-all-start = ((s32[8,1,20]{2,1,0:T(1,128)}), s32[8,1,20]{2,1,0:T(1,128)S(1)}, u32[]{:S(2)}, u32[]{:S(2)}) async-start(s32[8,1,20]{2,1,0:T(1,128)} %all_to_all.15), calls=%async_computation | async-start | bytes 8192 | tf_op jit(solution)/shard_map/all_to_all | solution.py:53
  15.7 1.5 and_select_fusion.2
  17.1 1.1 gather_fusion.5
  18.2 1.1 gather_fusion.2
  19.7 1.1 reshape.313
  20.8 6.1 %all-to-all-start.2 = ((bf16[8,20,2560]{2,1,0:T(8,128)(2,1)}), bf16[8,20,2560]{2,1,0:T(8,128)(2,1)S(1)}, u32[]{:S(2)}, u32[]{:S(2)}) async-start(bf16[8,20,2560]{2,1,0:T(8,128)(2,1)} %reshape.313), calls=%async_computation.2 | async-start | bytes 1966080 | tf_op jit(solution)/shard_map/all_to_all | solution.py:55
  26.9 1.1 reshape.309
  28.1 4.1 %scatter_custom_fusion.2 = s32[640]{0:T(1024)S(1)} fusion(s32[640]{0:T(1024)S(1)} %fusion.17, s32[640]{0:T(1024)S(1)} %iota.56, s32[]{:T(128)} %constant.39.clone.1), kind=kCustom, calls=%fused_computation.84 | custom fusion | bytes 2564 | tf_op jit(solution)/shard_map/scatter | solution.py:73
  32.4 15.0 %all-to-all-done.2 = bf16[8,20,2560]{2,1,0:T(8,128)(2,1)S(1)} async-done(((bf16[8,20,2560]{2,1,0:T(8,128)(2,1)}), bf16[8,20,2560]{2,1,0:T(8,128)(2,1)S(1)}, u32[]{:S(2)}, u32[]{:S(2)}) %all-to-all-start.2) | async-done | bytes 819232 | tf_op jit(solution)/shard_map/all_to_all | solution.py:55
  47.4 7.0 %all-to-all-start.1 = ((bf16[8,20,2560]{2,1,0:T(8,128)(2,1)}), bf16[8,20,2560]{2,1,0:T(8,128)(2,1)S(1)}, u32[]{:S(2)}, u32[]{:S(2)}) async-start(bf16[8,20,2560]{2,1,0:T(8,128)(2,1)} %reshape.309), calls=%async_computation.1 | async-start | bytes 1966080 | tf_op jit(solution)/shard_map/all_to_all | solution.py:52
  55.8 1.3 scatter_custom_fusion.1
  57.3 2.0 %gather_fusion.6 = bf16[160,2560]{1,0:T(8,128)(2,1)} fusion(bf16[160,2560]{1,0:T(8,128)(2,1)S(1)} %reshape.314, s32[1024]{0:T(1024)S(1)} %pad_clamp_fusion.6), kind=kCustom, calls=%fused_computation.4.clone | custom fusion | bytes 1639040 | tf_op jit(solution)/shard_map/jit(_take)/gather | solution.py:67
  59.3 16.2 %all-to-all-done.1 = bf16[8,20,2560]{2,1,0:T(8,128)(2,1)S(1)} async-done(((bf16[8,20,2560]{2,1,0:T(8,128)(2,1)}), bf16[8,20,2560]{2,1,0:T(8,128)(2,1)S(1)}, u32[]{:S(2)}, u32[]{:S(2)}) %all-to-all-start.1) | async-done | bytes 819232 | tf_op jit(solution)/shard_map/all_to_all | solution.py:52
  75.7 1.1 gather_fusion.3
  80.0 3.0 %gather_fusion.7 = bf16[640,640]{1,0:T(8,128)(2,1)S(1)} fusion(bf16[640,640]{0,1:T(8,128)(2,1)S(1)} %copy.43, s32[1024]{0:T(1024)S(1)} %pad_clamp_fusion.5), kind=kCustom, calls=%fused_computation.7.clone | custom fusion | bytes 1640960 | tf_op jit(solution)/shard_map/jit(_take)/gather | solution.py:68
  82.9 3.0 %gather_fusion.4 = bf16[640,640]{1,0:T(8,128)(2,1)S(1)} fusion(bf16[640,640]{0,1:T(8,128)(2,1)S(1)} %copy.42, s32[1024]{0:T(1024)S(1)} %pad_clamp_fusion.5), kind=kCustom, calls=%fused_computation.1.clone | custom fusion | bytes 1640960 | tf_op jit(solution)/shard_map/jit(_take)/gather | solution.py:68
  85.9 1.2 fusion.5
  87.1 1.2 subtract_convert_fusion
  89.3 3.0 %gather_fusion.8 = bf16[640,640]{1,0:T(8,128)(2,1)S(1)} fusion(bf16[640,640]{0,1:T(8,128)(2,1)S(1)} %copy.44, s32[1024]{0:T(1024)S(1)} %pad_clamp_fusion.4), kind=kCustom, calls=%fused_computation.8.clone | custom fusion | bytes 1640960 | tf_op jit(solution)/shard_map/jit(_take)/gather | solution.py:74
  93.9 1.1 gather_fusion.9
  95.3 1.1 reshape.317
  96.4 6.9 %all-to-all-start.3 = ((bf16[8,20,2560]{2,1,0:T(8,128)(2,1)}), bf16[8,20,2560]{2,1,0:T(8,128)(2,1)S(1)}, u32[]{:S(2)}, u32[]{:S(2)}) async-start(bf16[8,20,2560]{2,1,0:T(8,128)(2,1)} %reshape.317), calls=%async_computation.3 | async-start | bytes 1966080 | tf_op jit(solution)/shard_map/all_to_all | solution.py:78
  103.5 2.4 %fusion.1 = f32[640,640]{1,0:T(8,128)} fusion(f32[640]{0:T(1024)S(1)} %reduce, bf16[1,640,640]{2,1,0:T(8,128)(2,1)S(1)} %copy-done.7, pred[640]{0:T(1024)(128)(4,1)S(1)} %get-tuple-element.19, bf16[1,640,640]{2,1,0:T(8,128)(2,1)S(1)} %copy-done.5), kind=kOutput, calls=%fused_computation.30 | convolution fusion | flops 527155200 | bytes 3280000 | tf_op jit(solution)/shard_map/dot_general | solution.py:12
  105.8 18.8 %all-to-all-done.3 = bf16[8,20,2560]{2,1,0:T(8,128)(2,1)S(1)} async-done(((bf16[8,20,2560]{2,1,0:T(8,128)(2,1)}), bf16[8,20,2560]{2,1,0:T(8,128)(2,1)S(1)}, u32[]{:S(2)}, u32[]{:S(2)}) %all-to-all-start.3) | async-done | bytes 819232 | tf_op jit(solution)/shard_map/all_to_all | solution.py:78
  124.8 1.1 gather_fusion.10
  127.5 3.0 %gather_fusion.1 = bf16[640,640]{1,0:T(8,128)(2,1)S(1)} fusion(bf16[640,640]{1,0:T(8,128)(2,1)S(1)} %reshape.319, s32[1024]{0:T(1024)S(1)} %pad_clamp_fusion.1), kind=kCustom, calls=%fused_computation.12 | custom fusion | bytes 1640960 | tf_op jit(solution)/shard_map/jit(_take)/gather | solution.py:90
  132.5 3.0 %gather_fusion.12 = bf16[640,640]{1,0:T(8,128)(2,1)S(1)} fusion(bf16[640,640]{0,1:T(8,128)(2,1)S(1)} %copy.48, s32[1024]{0:T(1024)S(1)} %pad_clamp_fusion), kind=kCustom, calls=%fused_computation.10.clone | custom fusion | bytes 1640960 | tf_op jit(solution)/shard_map/jit(_take)/gather | solution.py:92
  135.5 1.3 copy.49
  136.8 3.0 %gather_fusion.11 = bf16[640,640]{1,0:T(8,128)(2,1)S(1)} fusion(bf16[640,640]{0,1:T(8,128)(2,1)S(1)} %copy.46, s32[1024]{0:T(1024)S(1)} %pad_clamp_fusion), kind=kCustom, calls=%fused_computation.9.clone | custom fusion | bytes 1640960 | tf_op jit(solution)/shard_map/jit(_take)/gather | solution.py:91
  140.7 5.7 %select_reduce_fusion = (f32[]{:T(128)}, f32[1,640,640]{2,1,0:T(8,128)}) fusion(bf16[640,640]{0,1:T(8,128)(2,1)} %copy.49, bf16[640,640]{0,1:T(8,128)(2,1)S(1)} %copy.47, pred[640]{0:T(1024)(128)(4,1)S(1)} %get-tuple-element.20, bf16[640,640]{1,0:T(8,128)(2,1)S(1)} %copy-done.2, bf16[640,640]{1,0:T(8,128)(2,1)S(1)} %reshape.319, ...), kind=kOutput, calls=%fused_computation.18 | convolution fusion | flops 534528000 | bytes 8195844 | tf_op jit(solution)/shard_map/dot_general | solution.py:12
  146.4 43.0 %psum.7 = f32[]{:T(128)} all-reduce(f32[]{:T(128)} %get-tuple-element.11), channel_id=1, replica_groups=mesh['chan'=8,'grp'=4] {'chan','grp'}, use_global_device_ids=true, to_apply=%region_5.8 | all-reduce | flops 1 | bytes 8 | tf_op jit(solution)/shard_map/psum | solution.py:100
  (95 shorter events, 19.3 us)
Async XLA Ops:
  0.6 2.8 %copy-start = (s32[1,160]{1,0:T(1,128)S(1)}, s32[1,160]{1,0:T(1,128)}, u32[]{:S(2)}) copy-start(s32[1,160]{1,0:T(1,128)} %param.19) | copy-start | bytes 1924
  0.6 14.0 %copy-start.6 = (bf16[1,640,640]{2,1,0:T(8,128)(2,1)S(1)}, bf16[1,640,640]{2,1,0:T(8,128)(2,1)}, u32[]{:S(2)}) copy-start(bf16[1,640,640]{2,1,0:T(8,128)(2,1)} %param.13) | copy-start | bytes 2457604
  5.1 10.1 %copy-start.4 = (bf16[1,640,640]{2,1,0:T(8,128)(2,1)S(1)}, bf16[1,640,640]{2,1,0:T(8,128)(2,1)}, u32[]{:S(2)}) copy-start(bf16[1,640,640]{2,1,0:T(8,128)(2,1)} %param.14) | copy-start | bytes 2457604
  5.8 15.0 %all-to-all-start = ((s32[8,1,20]{2,1,0:T(1,128)}), s32[8,1,20]{2,1,0:T(1,128)S(1)}, u32[]{:S(2)}, u32[]{:S(2)}) async-start(s32[8,1,20]{2,1,0:T(1,128)} %all_to_all.15), calls=%async_computation | async-start | bytes 8192 | tf_op jit(solution)/shard_map/all_to_all | solution.py:53
  19.6 7.3 %copy-start.9 = (s32[1,640]{1,0:T(1,128)S(1)}, s32[1,640]{1,0:T(1,128)}, u32[]{:S(2)}) copy-start(s32[1,640]{1,0:T(1,128)} %param.20) | copy-start | bytes 7684
  20.8 7.3 %copy-start.11 = (f32[1,640]{1,0:T(1,128)S(1)}, f32[1,640]{1,0:T(1,128)}, u32[]{:S(2)}) copy-start(f32[1,640]{1,0:T(1,128)} %param.16) | copy-start | bytes 7684
  20.8 26.6 %all-to-all-start.2 = ((bf16[8,20,2560]{2,1,0:T(8,128)(2,1)}), bf16[8,20,2560]{2,1,0:T(8,128)(2,1)S(1)}, u32[]{:S(2)}, u32[]{:S(2)}) async-start(bf16[8,20,2560]{2,1,0:T(8,128)(2,1)} %reshape.313), calls=%async_computation.2 | async-start | bytes 1966080 | tf_op jit(solution)/shard_map/all_to_all | solution.py:55
  47.4 28.1 %all-to-all-start.1 = ((bf16[8,20,2560]{2,1,0:T(8,128)(2,1)}), bf16[8,20,2560]{2,1,0:T(8,128)(2,1)S(1)}, u32[]{:S(2)}, u32[]{:S(2)}) async-start(bf16[8,20,2560]{2,1,0:T(8,128)(2,1)} %reshape.309), calls=%async_computation.1 | async-start | bytes 1966080 | tf_op jit(solution)/shard_map/all_to_all | solution.py:52
  75.7 1.1 copy-start.3
  95.2 8.1 %copy-start.12 = (f32[1,640]{1,0:T(1,128)S(1)}, f32[1,640]{1,0:T(1,128)}, u32[]{:S(2)}) copy-start(f32[1,640]{1,0:T(1,128)} %param.15) | copy-start | bytes 7684
  95.2 8.1 %copy-start.8 = (s32[1,160]{1,0:T(1,128)S(1)}, s32[1,160]{1,0:T(1,128)}, u32[]{:S(2)}) copy-start(s32[1,160]{1,0:T(1,128)} %param.18) | copy-start | bytes 1924
  95.3 8.2 %copy-start.10 = (s32[1,640]{1,0:T(1,128)S(1)}, s32[1,640]{1,0:T(1,128)}, u32[]{:S(2)}) copy-start(s32[1,640]{1,0:T(1,128)} %param.21) | copy-start | bytes 7684
  95.3 8.2 %copy-start.5 = (bf16[1,640,640]{2,1,0:T(8,128)(2,1)S(1)}, bf16[1,640,640]{2,1,0:T(8,128)(2,1)}, u32[]{:S(2)}) copy-start(bf16[1,640,640]{2,1,0:T(8,128)(2,1)} %param.14) | copy-start | bytes 2457604
  95.3 8.2 %copy-start.7 = (bf16[1,640,640]{2,1,0:T(8,128)(2,1)S(1)}, bf16[1,640,640]{2,1,0:T(8,128)(2,1)}, u32[]{:S(2)}) copy-start(bf16[1,640,640]{2,1,0:T(8,128)(2,1)} %param.13) | copy-start | bytes 2457604
  96.4 28.2 %all-to-all-start.3 = ((bf16[8,20,2560]{2,1,0:T(8,128)(2,1)}), bf16[8,20,2560]{2,1,0:T(8,128)(2,1)S(1)}, u32[]{:S(2)}, u32[]{:S(2)}) async-start(bf16[8,20,2560]{2,1,0:T(8,128)(2,1)} %reshape.317), calls=%async_computation.3 | async-start | bytes 1966080 | tf_op jit(solution)/shard_map/all_to_all | solution.py:78
  130.5 0.9 copy-start.1
  136.8 3.9 %copy-start.2 = (bf16[640,640]{1,0:T(8,128)(2,1)S(1)}, bf16[640,640]{1,0:T(8,128)(2,1)}, u32[]{:S(2)}) copy-start(bf16[640,640]{1,0:T(8,128)(2,1)} %copy-done.1) | copy-start | bytes 2457604
where the time goes:
time: 192 us; the launch traced here: 191 us
  local copies, waits for them, and re-layouts  51.8 us (27%)
  waiting for transfers between devices  50 us (26%)
  blocking collectives  43 us (22%)
  starting transfers between devices  26.3 us (14%)
  matrix products  10.5 us (5%)
  other arithmetic  5.94 us (3%)
  between operations  3.71 us (2%)
    psum x1, blocking collectives, on_device(): energy_flow = 0.25 * lax.psum(jnp.trace(ladder), ('chan', 'grp'))  43 us
    all_to_all x1, waiting for transfers between devices, on_device(): lax.all_to_all(picked.reshape(peer_count, slot_count, row_len), 'chan', s...  18.8 us
    all_to_all x1, waiting for transfers between devices, on_device(): lax.all_to_all(pack_rows(gen_masked), 'chan', split_axis=0, concat_axis=0...  16.2 us
    all_to_all x1, waiting for transfers between devices, on_device(): lax.all_to_all(pack_rows(ham_masked), 'chan', split_axis=0, concat_axis=0...  15 us
    all_to_all x1, starting transfers between devices, on_device(): lax.all_to_all(pack_rows(gen_masked), 'chan', split_axis=0, concat_axis=0...  7.01 us
    all_to_all x1, starting transfers between devices, on_device(): lax.all_to_all(picked.reshape(peer_count, slot_count, row_len), 'chan', s...  6.91 us
    dot_general x2, matrix products, commutator(): jnp.dot(right, scaled_rows(scale, left), preferred_element_type=jnp.float32)  6.89 us
    all_to_all x1, starting transfers between devices, on_device(): lax.all_to_all(positions, 'chan', split_axis=0, concat_axis=0, tiled=True)  6.22 us
  transfers between devices with their start and end apart: 4, of which 3 were waited for; matrix products, arithmetic and copies ran while one was open for 11% of the time, Pallas kernels for 0%

commit v1 on v0

--- a/solution.py
+++ b/solution.py
@@ -2,6 +2,28 @@
 import jax.numpy as jnp
 from jax import lax
 from jax.sharding import PartitionSpec as P
+
+
+def split_up(value, dim, size):
+    before, after = (value.shape[:dim], value.shape[dim + 1 :])
+    return jnp.moveaxis(value.reshape(*before, size, -1, *after), dim, 0)
+
+
+def laid_out(blocks, dim):
+    blocks = jnp.moveaxis(blocks, 0, dim)
+    dims = blocks.shape
+    return blocks.reshape(*dims[:dim], dims[dim] * dims[dim + 1], *dims[dim + 2 :])
+
+
+def exchange_in_pairs(array, axis, split_dim, concat_dim):
+    size, position = (lax.axis_size(axis), lax.axis_index(axis))
+    pieces = split_up(array, split_dim, size)
+    outs = [pieces[position]]
+    for lap in range(1, size):
+        sent = pieces[position ^ lap]
+        outs.append(lax.ppermute(sent, axis, [(i, i ^ lap) for i in range(size)]))
+    pieces = jnp.stack(outs)[position ^ jnp.arange(size)]
+    return laid_out(pieces, concat_dim)
 
 
 def scaled_rows(scale, matrix):
@@ -52,9 +74,7 @@
         lax.all_to_all(pack_rows(gen_masked), "chan", split_axis=0, concat_axis=0, tiled=True),
         lax.all_to_all(positions, "chan", split_axis=0, concat_axis=0, tiled=True),
     )
-    ham_recv = lax.all_to_all(
-        pack_rows(ham_masked), "chan", split_axis=0, concat_axis=0, tiled=True
-    )
+    ham_recv = exchange_in_pairs(pack_rows(ham_masked), "chan", 0, 0)
     flat_pos = got_pos.reshape(-1)
     arrival = (
         jnp.zeros((sub_count,), jnp.int32)

time: 192 us -> 183 us (0.953)
  waiting for transfers between devices: 50 us -> 38.5 us
  starting transfers between devices: 26.3 us -> 30 us
    ppermute x0 -> x7, waiting for transfers between devices: none -> 20.3 us  [exchange_in_pairs(): outs.append(lax.ppermute(sent, axis, [(i, i ^ lap) for i in range(size)]))]
    all_to_all x1, waiting for transfers between devices: 16.2 us -> 0.01 us  [on_device(): lax.all_to_all(pack_rows(gen_masked), 'chan', split_axis=0, concat_axis=0...]
    all_to_all x1 -> x0, waiting for transfers between devices: 15 us -> none  [on_device(): lax.all_to_all(pack_rows(ham_masked), 'chan', split_axis=0, concat_axis=0...]
    ppermute x0 -> x7, starting transfers between devices: none -> 8.46 us  [exchange_in_pairs(): outs.append(lax.ppermute(sent, axis, [(i, i ^ lap) for i in range(size)]))]
    all_to_all x1 -> x0, starting transfers between devices: 6.13 us -> none  [on_device(): lax.all_to_all(pack_rows(ham_masked), 'chan', split_axis=0, concat_axis=0...]
  transfers between devices with their start and end apart: 4 -> 10, of which waited for: 3 -> 3; matrix products, arithmetic and copies ran while one was open for 11% -> 11% of each run, Pallas kernels for 0% -> 0%
where the time goes in v1:
time: 183 us; the launch traced here: 182 us
  local copies, waits for them, and re-layouts  51.4 us (28%)
  blocking collectives  43 us (23%)
  waiting for transfers between devices  38.5 us (21%)
  starting transfers between devices  30 us (16%)
  matrix products  10.5 us (6%)
  other arithmetic  5.27 us (3%)
  between operations  3.86 us (2%)
    psum x1, blocking collectives, on_device(): energy_flow = 0.25 * lax.psum(jnp.trace(ladder), ('chan', 'grp'))  43 us
    ppermute x7, waiting for transfers between devices, exchange_in_pairs(): outs.append(lax.ppermute(sent, axis, [(i, i ^ lap) for i in range(size)]))  20.3 us
    all_to_all x1, waiting for transfers between devices, on_device(): lax.all_to_all(picked.reshape(peer_count, slot_count, row_len), 'chan', s...  18.1 us
    all_to_all x1, starting transfers between devices, on_device(): lax.all_to_all(picked.reshape(peer_count, slot_count, row_len), 'chan', s...  8.74 us
    ppermute x7, starting transfers between devices, exchange_in_pairs(): outs.append(lax.ppermute(sent, axis, [(i, i ^ lap) for i in range(size)]))  8.46 us
    dot_general x2, matrix products, commutator(): jnp.dot(right, scaled_rows(scale, left), preferred_element_type=jnp.float32)  6.89 us
    all_to_all x1, starting transfers between devices, on_device(): lax.all_to_all(pack_rows(gen_masked), 'chan', split_axis=0, concat_axis=0...  6.57 us
    all_to_all x1, starting transfers between devices, on_device(): lax.all_to_all(positions, 'chan', split_axis=0, concat_axis=0, tiled=True)  6.22 us
  transfers between devices with their start and end apart: 10, of which 3 were waited for; matrix products, arithmetic and copies ran while one was open for 11% of the time, Pallas kernels for 0%

profile of v1, /device:TPU:12, one launch (start us, length us, event | category | flops | bytes accessed | tf_op | source)
XLA Modules:
  0.0 182.4 jit_solution(9145631670829987743)
XLA Ops:
  3.4 1.6 gather_fusion
  5.8 6.2 %all-to-all-start = ((s32[8,1,20]{2,1,0:T(1,128)}), s32[8,1,20]{2,1,0:T(1,128)S(1)}, u32[]{:S(2)}, u32[]{:S(2)}) async-start(s32[8,1,20]{2,1,0:T(1,128)} %all_to_all.12), calls=%async_computation | async-start | bytes 8192 | tf_op jit(solution)/shard_map/all_to_all | solution.py:75
  14.9 1.5 and_select_fusion.2
  16.4 1.1 gather_fusion.6
  17.5 1.1 gather_fusion.3
  20.0 1.5 collective-permute-start.6
  22.0 5.1 %collective-permute-start.4 = (bf16[1,20,2560]{2,1,0:T(8,128)(2,1)S(1)}, bf16[1,20,2560]{2,1,0:T(8,128)(2,1)S(1)}, u32[]{:S(2)}, u32[]{:S(2)}) collective-permute-start(bf16[1,20,2560]{2,1,0:T(8,128)(2,1)S(1)} %get-tuple-element.15), channel_id=1, source_target_pairs={{0,20},{4,16},{8,28},{12,24},{16,4},{20,0},{24,12},{28,8},{1,21},{... | collective-permute-start | bytes 307208 | tf_op jit(solution)/shard_map/ppermute | solution.py:24
  27.8 4.1 %scatter_custom_fusion.2 = s32[640]{0:T(1024)S(1)} fusion(s32[640]{0:T(1024)S(1)} %get-tuple-element.27, s32[640]{0:T(1024)S(1)} %iota.61, s32[]{:T(128)} %constant.25.clone.1), kind=kCustom, calls=%fused_computation.102 | custom fusion | bytes 2564 | tf_op jit(solution)/shard_map/scatter | solution.py:93
  32.0 1.1 reshape.319
  33.1 6.6 %all-to-all-start.1 = ((bf16[8,20,2560]{2,1,0:T(8,128)(2,1)}), bf16[8,20,2560]{2,1,0:T(8,128)(2,1)S(1)}, u32[]{:S(2)}, u32[]{:S(2)}) async-start(bf16[8,20,2560]{2,1,0:T(8,128)(2,1)} %reshape.319), calls=%async_computation.1 | async-start | bytes 1966080 | tf_op jit(solution)/shard_map/all_to_all | solution.py:74
  41.0 1.3 scatter_custom_fusion.1
  43.1 14.7 %collective-permute-done.1 = bf16[1,20,2560]{2,1,0:T(8,128)(2,1)S(1)} collective-permute-done((bf16[1,20,2560]{2,1,0:T(8,128)(2,1)}, bf16[1,20,2560]{2,1,0:T(8,128)(2,1)S(1)}, u32[]{:S(2)}, u32[]{:S(2)}) %collective-permute-start.1) | collective-permute-done | bytes 102432 | tf_op jit(solution)/shard_map/ppermute | solution.py:24
  58.0 5.6 %collective-permute-done.2 = bf16[1,20,2560]{2,1,0:T(8,128)(2,1)S(1)} collective-permute-done((bf16[1,20,2560]{2,1,0:T(8,128)(2,1)S(1)}, bf16[1,20,2560]{2,1,0:T(8,128)(2,1)S(1)}, u32[]{:S(2)}, u32[]{:S(2)}) %collective-permute-start.2) | collective-permute-done | bytes 102432 | tf_op jit(solution)/shard_map/ppermute | solution.py:24
  64.6 1.1 gather_fusion.7
  65.8 1.1 gather_fusion.4
  70.1 3.0 %gather_fusion.8 = bf16[640,640]{1,0:T(8,128)(2,1)S(1)} fusion(bf16[640,640]{0,1:T(8,128)(2,1)S(1)} %copy.43, s32[1024]{0:T(1024)S(1)} %pad_clamp_fusion.6), kind=kCustom, calls=%fused_computation.7.clone | custom fusion | bytes 1640960 | tf_op jit(solution)/shard_map/jit(_take)/gather | solution.py:88
  73.0 3.0 %gather_fusion.5 = bf16[640,640]{1,0:T(8,128)(2,1)S(1)} fusion(bf16[640,640]{0,1:T(8,128)(2,1)S(1)} %copy.42, s32[1024]{0:T(1024)S(1)} %pad_clamp_fusion.6), kind=kCustom, calls=%fused_computation.1.clone | custom fusion | bytes 1640960 | tf_op jit(solution)/shard_map/jit(_take)/gather | solution.py:88
  76.0 1.2 fusion.5
  77.2 1.2 subtract_convert_fusion
  79.4 3.0 %gather_fusion.9 = bf16[640,640]{1,0:T(8,128)(2,1)S(1)} fusion(bf16[640,640]{0,1:T(8,128)(2,1)S(1)} %copy.44, s32[1024]{0:T(1024)S(1)} %pad_clamp_fusion.4), kind=kCustom, calls=%fused_computation.8.clone | custom fusion | bytes 1640960 | tf_op jit(solution)/shard_map/jit(_take)/gather | solution.py:94
  84.0 1.1 gather_fusion.10
  85.4 1.1 reshape.325
  86.5 8.7 %all-to-all-start.2 = ((bf16[8,20,2560]{2,1,0:T(8,128)(2,1)}), bf16[8,20,2560]{2,1,0:T(8,128)(2,1)S(1)}, u32[]{:S(2)}, u32[]{:S(2)}) async-start(bf16[8,20,2560]{2,1,0:T(8,128)(2,1)} %reshape.325), calls=%async_computation.2 | async-start | bytes 1966080 | tf_op jit(solution)/shard_map/all_to_all | solution.py:98
  95.4 2.4 %fusion.1 = f32[640,640]{1,0:T(8,128)} fusion(f32[640]{0:T(1024)S(1)} %reduce, bf16[1,640,640]{2,1,0:T(8,128)(2,1)S(1)} %copy-done.6, pred[640]{0:T(1024)(128)(4,1)S(1)} %iota_compare_fusion.2, bf16[1,640,640]{2,1,0:T(8,128)(2,1)S(1)} %copy-done.4), kind=kOutput, calls=%fused_computation.31 | convolution fusion | flops 527155200 | bytes 3280000 | tf_op jit(solution)/shard_map/dot_general | solution.py:34
  97.7 18.1 %all-to-all-done.2 = bf16[8,20,2560]{2,1,0:T(8,128)(2,1)S(1)} async-done(((bf16[8,20,2560]{2,1,0:T(8,128)(2,1)}), bf16[8,20,2560]{2,1,0:T(8,128)(2,1)S(1)}, u32[]{:S(2)}, u32[]{:S(2)}) %all-to-all-start.2) | async-done | bytes 819232 | tf_op jit(solution)/shard_map/all_to_all | solution.py:98
  116.0 1.1 gather_fusion.11
  118.7 3.0 %gather_fusion.2 = bf16[640,640]{1,0:T(8,128)(2,1)S(1)} fusion(bf16[640,640]{1,0:T(8,128)(2,1)S(1)} %reshape.327, s32[1024]{0:T(1024)S(1)} %pad_clamp_fusion.1), kind=kCustom, calls=%fused_computation.13 | custom fusion | bytes 1640960 | tf_op jit(solution)/shard_map/jit(_take)/gather | solution.py:110
  123.8 3.0 %gather_fusion.13 = bf16[640,640]{1,0:T(8,128)(2,1)S(1)} fusion(bf16[640,640]{0,1:T(8,128)(2,1)S(1)} %copy.48, s32[1024]{0:T(1024)S(1)} %get-tuple-element.29), kind=kCustom, calls=%fused_computation.10.clone | custom fusion | bytes 1640960 | tf_op jit(solution)/shard_map/jit(_take)/gather | solution.py:112
  126.7 1.3 copy.49
  128.0 3.0 %gather_fusion.12 = bf16[640,640]{1,0:T(8,128)(2,1)S(1)} fusion(bf16[640,640]{0,1:T(8,128)(2,1)S(1)} %copy.46, s32[1024]{0:T(1024)S(1)} %get-tuple-element.29), kind=kCustom, calls=%fused_computation.9.clone | custom fusion | bytes 1640960 | tf_op jit(solution)/shard_map/jit(_take)/gather | solution.py:111
  132.0 5.7 %select_reduce_fusion = (f32[]{:T(128)}, f32[1,640,640]{2,1,0:T(8,128)}) fusion(bf16[640,640]{0,1:T(8,128)(2,1)} %copy.49, bf16[640,640]{0,1:T(8,128)(2,1)S(1)} %copy.47, pred[640]{0:T(1024)(128)(4,1)S(1)} %compare_and_fusion.2, bf16[640,640]{1,0:T(8,128)(2,1)S(1)} %copy-done.2, bf16[640,640]{1,0:T(8,128)(2,1)S(1)} %reshape.327, ...), kind=kOutput, calls=%fused_computation.19 | convolution fusion | flops 534528000 | bytes 8195844 | tf_op jit(solution)/shard_map/dot_general | solution.py:34
  137.6 43.0 %psum.7 = f32[]{:T(128)} all-reduce(f32[]{:T(128)} %get-tuple-element.11), channel_id=1, replica_groups=mesh['chan'=8,'grp'=4] {'chan','grp'}, use_global_device_ids=true, to_apply=%region_5.8 | all-reduce | flops 1 | bytes 8 | tf_op jit(solution)/shard_map/psum | solution.py:120
  (115 shorter events, 22.2 us)
Async XLA Ops:
  0.6 2.8 %copy-start = (s32[1,160]{1,0:T(1,128)S(1)}, s32[1,160]{1,0:T(1,128)}, u32[]{:S(2)}) copy-start(s32[1,160]{1,0:T(1,128)} %param.19) | copy-start | bytes 1924
  0.6 13.3 %copy-start.5 = (bf16[1,640,640]{2,1,0:T(8,128)(2,1)S(1)}, bf16[1,640,640]{2,1,0:T(8,128)(2,1)}, u32[]{:S(2)}) copy-start(bf16[1,640,640]{2,1,0:T(8,128)(2,1)} %param.13) | copy-start | bytes 2457604
  5.1 9.4 %copy-start.3 = (bf16[1,640,640]{2,1,0:T(8,128)(2,1)S(1)}, bf16[1,640,640]{2,1,0:T(8,128)(2,1)}, u32[]{:S(2)}) copy-start(bf16[1,640,640]{2,1,0:T(8,128)(2,1)} %param.14) | copy-start | bytes 2457604
  5.8 27.3 %all-to-all-start = ((s32[8,1,20]{2,1,0:T(1,128)}), s32[8,1,20]{2,1,0:T(1,128)S(1)}, u32[]{:S(2)}, u32[]{:S(2)}) async-start(s32[8,1,20]{2,1,0:T(1,128)} %all_to_all.12), calls=%async_computation | async-start | bytes 8192 | tf_op jit(solution)/shard_map/all_to_all | solution.py:75
  18.9 8.7 %copy-start.8 = (s32[1,640]{1,0:T(1,128)S(1)}, s32[1,640]{1,0:T(1,128)}, u32[]{:S(2)}) copy-start(s32[1,640]{1,0:T(1,128)} %param.20) | copy-start | bytes 7684
  18.9 8.8 %copy-start.9 = (s32[1,640]{1,0:T(1,128)S(1)}, s32[1,640]{1,0:T(1,128)}, u32[]{:S(2)}) copy-start(s32[1,640]{1,0:T(1,128)} %param.21) | copy-start | bytes 7684
  19.2 13.9 %copy-start.10 = (f32[1,640]{1,0:T(1,128)S(1)}, f32[1,640]{1,0:T(1,128)}, u32[]{:S(2)}) copy-start(f32[1,640]{1,0:T(1,128)} %param.16) | copy-start | bytes 7684
  20.0 43.7 %collective-permute-start.6 = (bf16[1,20,2560]{2,1,0:T(8,128)(2,1)S(1)}, bf16[1,20,2560]{2,1,0:T(8,128)(2,1)S(1)}, u32[]{:S(2)}, u32[]{:S(2)}) collective-permute-start(bf16[1,20,2560]{2,1,0:T(8,128)(2,1)S(1)} %get-tuple-element.13), channel_id=1, source_target_pairs={{0,28},{4,24},{8,20},{12,16},{16,12},{20,8},{24,4},{28,0},{1,29},{... | collective-permute-start | bytes 307208 | tf_op jit(solution)/shard_map/ppermute | solution.py:24
  21.5 42.2 %collective-permute-start.5 = (bf16[1,20,2560]{2,1,0:T(8,128)(2,1)S(1)}, bf16[1,20,2560]{2,1,0:T(8,128)(2,1)S(1)}, u32[]{:S(2)}, u32[]{:S(2)}) collective-permute-start(bf16[1,20,2560]{2,1,0:T(8,128)(2,1)S(1)} %get-tuple-element.14), channel_id=1, source_target_pairs={{0,24},{4,28},{8,16},{12,20},{16,8},{20,12},{24,0},{28,4},{1,25},{... | collective-permute-start | bytes 307208 | tf_op jit(solution)/shard_map/ppermute | solution.py:24
  22.0 41.7 %collective-permute-start.4 = (bf16[1,20,2560]{2,1,0:T(8,128)(2,1)S(1)}, bf16[1,20,2560]{2,1,0:T(8,128)(2,1)S(1)}, u32[]{:S(2)}, u32[]{:S(2)}) collective-permute-start(bf16[1,20,2560]{2,1,0:T(8,128)(2,1)S(1)} %get-tuple-element.15), channel_id=1, source_target_pairs={{0,20},{4,16},{8,28},{12,24},{16,4},{20,0},{24,12},{28,8},{1,21},{... | collective-permute-start | bytes 307208 | tf_op jit(solution)/shard_map/ppermute | solution.py:24
  27.1 36.6 %collective-permute-start.3 = (bf16[1,20,2560]{2,1,0:T(8,128)(2,1)S(1)}, bf16[1,20,2560]{2,1,0:T(8,128)(2,1)S(1)}, u32[]{:S(2)}, u32[]{:S(2)}) collective-permute-start(bf16[1,20,2560]{2,1,0:T(8,128)(2,1)S(1)} %get-tuple-element.16), channel_id=1, source_target_pairs={{0,16},{4,20},{8,24},{12,28},{16,0},{20,4},{24,8},{28,12},{1,17},{... | collective-permute-start | bytes 307208 | tf_op jit(solution)/shard_map/ppermute | solution.py:24
  27.1 15.4 %collective-permute-start = (bf16[1,20,2560]{2,1,0:T(8,128)(2,1)}, bf16[1,20,2560]{2,1,0:T(8,128)(2,1)S(1)}, u32[]{:S(2)}, u32[]{:S(2)}) collective-permute-start(bf16[1,20,2560]{2,1,0:T(8,128)(2,1)} %get-tuple-element.19), channel_id=1, source_target_pairs={{0,4},{4,0},{8,12},{12,8},{16,20},{20,16},{24,28},{28,24},{1,5},{5... | collective-permute-start | bytes 307208 | tf_op jit(solution)/shard_map/ppermute | solution.py:24
  33.1 32.6 %all-to-all-start.1 = ((bf16[8,20,2560]{2,1,0:T(8,128)(2,1)}), bf16[8,20,2560]{2,1,0:T(8,128)(2,1)S(1)}, u32[]{:S(2)}, u32[]{:S(2)}) async-start(bf16[8,20,2560]{2,1,0:T(8,128)(2,1)} %reshape.319), calls=%async_computation.1 | async-start | bytes 1966080 | tf_op jit(solution)/shard_map/all_to_all | solution.py:74
  42.5 15.3 %collective-permute-start.1 = (bf16[1,20,2560]{2,1,0:T(8,128)(2,1)}, bf16[1,20,2560]{2,1,0:T(8,128)(2,1)S(1)}, u32[]{:S(2)}, u32[]{:S(2)}) collective-permute-start(bf16[1,20,2560]{2,1,0:T(8,128)(2,1)} %get-tuple-element.18), channel_id=1, source_target_pairs={{0,8},{4,12},{8,0},{12,4},{16,24},{20,28},{24,16},{28,20},{1,9},{5... | collective-permute-start | bytes 307208 | tf_op jit(solution)/shard_map/ppermute | solution.py:24
  57.9 5.8 %collective-permute-start.2 = (bf16[1,20,2560]{2,1,0:T(8,128)(2,1)S(1)}, bf16[1,20,2560]{2,1,0:T(8,128)(2,1)S(1)}, u32[]{:S(2)}, u32[]{:S(2)}) collective-permute-start(bf16[1,20,2560]{2,1,0:T(8,128)(2,1)S(1)} %get-tuple-element.17), channel_id=1, source_target_pairs={{0,12},{4,8},{8,4},{12,0},{16,28},{20,24},{24,20},{28,16},{1,13},{... | collective-permute-start | bytes 307208 | tf_op jit(solution)/shard_map/ppermute | solution.py:24
  85.3 9.9 %copy-start.11 = (f32[1,640]{1,0:T(1,128)S(1)}, f32[1,640]{1,0:T(1,128)}, u32[]{:S(2)}) copy-start(f32[1,640]{1,0:T(1,128)} %param.15) | copy-start | bytes 7684
  85.4 9.9 %copy-start.7 = (s32[1,160]{1,0:T(1,128)S(1)}, s32[1,160]{1,0:T(1,128)}, u32[]{:S(2)}) copy-start(s32[1,160]{1,0:T(1,128)} %param.18) | copy-start | bytes 1924
  85.4 10.0 %copy-start.4 = (bf16[1,640,640]{2,1,0:T(8,128)(2,1)S(1)}, bf16[1,640,640]{2,1,0:T(8,128)(2,1)}, u32[]{:S(2)}) copy-start(bf16[1,640,640]{2,1,0:T(8,128)(2,1)} %param.14) | copy-start | bytes 2457604
  85.4 10.0 %copy-start.6 = (bf16[1,640,640]{2,1,0:T(8,128)(2,1)S(1)}, bf16[1,640,640]{2,1,0:T(8,128)(2,1)}, u32[]{:S(2)}) copy-start(bf16[1,640,640]{2,1,0:T(8,128)(2,1)} %param.13) | copy-start | bytes 2457604
  86.5 29.3 %all-to-all-start.2 = ((bf16[8,20,2560]{2,1,0:T(8,128)(2,1)}), bf16[8,20,2560]{2,1,0:T(8,128)(2,1)S(1)}, u32[]{:S(2)}, u32[]{:S(2)}) async-start(bf16[8,20,2560]{2,1,0:T(8,128)(2,1)} %reshape.325), calls=%async_computation.2 | async-start | bytes 1966080 | tf_op jit(solution)/shard_map/all_to_all | solution.py:98
  121.7 0.9 copy-start.1
  128.0 3.9 %copy-start.2 = (bf16[640,640]{1,0:T(8,128)(2,1)S(1)}, bf16[640,640]{1,0:T(8,128)(2,1)}, u32[]{:S(2)}) copy-start(bf16[640,640]{1,0:T(8,128)(2,1)} %copy-done.1) | copy-start | bytes 2457604
